TPU v7x, 32 devices: a whole 2x2x4 slice. The times are simulated.
32 devices in a mesh: dp: 2 (over x), fsdp: 8 (over z, y), seq: 2 (over core).
Axes of the slice: x: 2, y: 2, z: 4, core: 2. Of those that a mesh axis runs over, the one named last changes fastest.
Arguments:
- tokens_in: bfloat16 [16, 1040, 1024], P(('dp', 'fsdp'), 'seq'), may hold values from -6 to 6
- key_mask: int32 [16, 1040], P(('dp', 'fsdp')), may hold values from 0 to 1, as said below
- attn_weights: bfloat16 [2, 1024, 4096], P(None, 'fsdp')
- mlp_weights: bfloat16 [2, 1024, 8192], P(None, 'fsdp')
- vectors: bfloat16 [2, 14, 1024], P(None, None, 'fsdp')
- cotangent: bfloat16 [16, 1040, 1024], P(('dp', 'fsdp'), 'seq'), may hold values from -6 to 6
- first_attn: float32 [2, 1024, 4096], P(None, 'fsdp'), may hold values from -40 to 40
- second_attn: float32 [2, 1024, 4096], P(None, 'fsdp'), may hold values from 0.832 to 8.32
- first_mlp: float32 [2, 1024, 8192], P(None, 'fsdp'), may hold values from -40 to 40
- second_mlp: float32 [2, 1024, 8192], P(None, 'fsdp'), may hold values from 0.832 to 8.32
- first_vec: float32 [2, 14, 1024], P(None, None, 'fsdp'), may hold values from -80 to 80
- second_vec: float32 [2, 14, 1024], P(None, None, 'fsdp'), may hold values from 3.328 to 33.28
Outputs:
- tokens_out: float32 [16, 1040, 1024], P(('dp', 'fsdp'), 'seq')
- grad_tokens: float32 [16, 1040, 1024], P(('dp', 'fsdp'), 'seq')
- grad_attn: float32 [2, 1024, 4096], P(None, 'fsdp')
- grad_mlp: float32 [2, 1024, 8192], P(None, 'fsdp')
- grad_vectors: float32 [2, 14, 1024], P(None, None, 'fsdp')
- step_attn: float32 [2, 1024, 4096], P(None, 'fsdp')
- step_mlp: float32 [2, 1024, 8192], P(None, 'fsdp')
- step_vectors: float32 [2, 14, 1024], P(None, None, 'fsdp')
- new_first_attn: float32 [2, 1024, 4096], P(None, 'fsdp')
- new_second_attn: float32 [2, 1024, 4096], P(None, 'fsdp')
- new_first_mlp: float32 [2, 1024, 8192], P(None, 'fsdp')
- new_second_mlp: float32 [2, 1024, 8192], P(None, 'fsdp')
- new_first_vec: float32 [2, 14, 1024], P(None, None, 'fsdp')
- new_second_vec: float32 [2, 14, 1024], P(None, None, 'fsdp')
Inputs may be any that keep to these rules, and one draw needn't show every extreme that they name: `key_mask`: each image's row is 1 on its first slots and 0 on the rest; at least 910 ones and at least one 0 in every row.
All inputs are finite; a program needn't handle non-finite values.
Results may differ from a plain program's by a relative error of at most 0.023.
Values may be sent and summed in bfloat16 or wider, within the bound.
No kernel may reach another device: no remote copies, remote signals or barrier semaphores. Data moves between devices by JAX's collectives and lax.ppermute only.
A program may use at most 320 MiB of HBM per device.

v0:
```python
import jax
import jax.numpy as jnp
from jax import lax
from jax.sharding import PartitionSpec as P

HD = 64
norm_eps = 1e-06
neg_large = -1e30
beta_first = 0.9
beta_second = 0.999
adam_eps = 1e-08
decay_rate = 0.05
rate_matrix = 0.01
rate_vector = 0.05
step_count = 10.0


def layer_norm(values, norm_gain, norm_shift):
    center = values - jnp.mean(values, axis=-1, keepdims=True)
    spread = jnp.mean(center * center, axis=-1, keepdims=True)
    return center * lax.rsqrt(spread + norm_eps) * norm_gain + norm_shift


def gelu_exact(values):
    return jax.nn.gelu(values, approximate=False)


def contract_last(left_side, right_side):
    return lax.dot_general(
        left_side,
        right_side,
        (((left_side.ndim - 1,), (1,)), ((), ())),
        preferred_element_type=jnp.float32,
    )


def contract_rows(left_side, right_side):
    return lax.dot_general(
        left_side, right_side, (((0, 1), (0, 1)), ((), ())), preferred_element_type=jnp.float32
    )


def masked_scores(query_rows, key_rows, valid_keys):
    scores = contract_last(query_rows, key_rows) * query_rows.shape[-1] ** (-0.5)
    return jnp.where(valid_keys[None, :] > 0, scores, neg_large)


def attend_item(item_set):
    query_rows, key_rows, value_rows, valid_keys = item_set
    scores = masked_scores(query_rows, key_rows, valid_keys)
    row_top = jnp.max(scores, axis=-1, keepdims=True)
    exp_terms = jnp.exp(scores - row_top)
    row_total = jnp.sum(exp_terms, axis=-1, keepdims=True)
    attention = (exp_terms / row_total).astype(jnp.bfloat16)
    mixed_rows = jnp.dot(attention, value_rows, preferred_element_type=jnp.float32)
    return (mixed_rows.astype(jnp.bfloat16), row_top[:, 0] + jnp.log(row_total[:, 0]))


def attend_back(item_set):
    query_rows, key_rows, value_rows, valid_keys, log_total, grad_rows = item_set
    score_scale = query_rows.shape[-1] ** (-0.5)
    scores = masked_scores(query_rows, key_rows, valid_keys)
    attention = jnp.exp(scores - log_total[:, None])
    grad_value = lax.dot_general(
        attention.astype(jnp.bfloat16),
        grad_rows,
        (((0,), (0,)), ((), ())),
        preferred_element_type=jnp.float32,
    )
    grad_attention = contract_last(grad_rows, value_rows)
    inner_sum = jnp.sum(attention * grad_attention, axis=-1, keepdims=True)
    grad_scores = (attention * (grad_attention - inner_sum)).astype(jnp.bfloat16)
    grad_query = jnp.dot(grad_scores, key_rows, preferred_element_type=jnp.float32) * score_scale
    grad_key = (
        lax.dot_general(
            grad_scores, query_rows, (((0,), (0,)), ((), ())), preferred_element_type=jnp.float32
        )
        * score_scale
    )
    return jnp.stack([grad_query, grad_key, grad_value]).astype(jnp.bfloat16)


def forward_layer(inputs, mask_heads, attn_full, mlp_full, vectors_full):
    model_width = attn_full.shape[0]
    hidden = mlp_full.shape[1] // 2
    vec_rows = vectors_full.astype(jnp.float32)
    n_seq = lax.axis_size("seq")
    images, token_rows, _ = inputs.shape
    length = token_rows * n_seq
    group_width = model_width // n_seq
    per_group = group_width // HD
    normed = layer_norm(inputs, vec_rows[0], vec_rows[1]).astype(jnp.bfloat16)
    bias_qkv = jnp.concatenate([vec_rows[2], jnp.zeros_like(vec_rows[2]), vec_rows[3]])
    qkv = (
        jnp.dot(normed, attn_full[:, : 3 * model_width], preferred_element_type=jnp.float32)
        + bias_qkv
    ).astype(jnp.bfloat16)
    heads = lax.all_to_all(
        qkv.reshape(images, token_rows, 3, n_seq, group_width),
        "seq",
        split_axis=3,
        concat_axis=1,
        tiled=True,
    )
    stacked = (
        heads.reshape(images, length, 3, per_group, HD)
        .transpose(2, 0, 3, 1, 4)
        .reshape(3, images * per_group, length, HD)
    )
    mixed_items, log_total = lax.map(attend_item, (stacked[0], stacked[1], stacked[2], mask_heads))
    mixed_heads = (
        mixed_items.reshape(images, per_group, length, HD)
        .transpose(0, 2, 1, 3)
        .reshape(images, length, 1, group_width)
    )
    mixed_rows = lax.all_to_all(
        mixed_heads, "seq", split_axis=1, concat_axis=2, tiled=True
    ).reshape(images, token_rows, model_width)
    branch = contract_last(mixed_rows, attn_full[:, 3 * model_width :]) + vec_rows[4]
    middle = inputs + vec_rows[5] * branch
    normed_two = layer_norm(middle, vec_rows[6], vec_rows[7]).astype(jnp.bfloat16)
    pre_act = jnp.dot(
        normed_two, mlp_full[:, :hidden], preferred_element_type=jnp.float32
    ) + vec_rows[10:].reshape(hidden)
    active = gelu_exact(pre_act).astype(jnp.bfloat16)
    mlp_out = contract_last(active, mlp_full[:, hidden:]) + vec_rows[8]
    output = middle + vec_rows[9] * mlp_out
    saved_set = (
        inputs,
        normed,
        stacked,
        log_total,
        mixed_rows,
        branch,
        middle,
        normed_two,
        pre_act,
        active,
        mlp_out,
    )
    return (output, saved_set)


def backward_layer(upstream, saved_set, attn_full, mlp_full, vectors_full, mask_heads):
    (
        inputs,
        normed,
        stacked,
        log_total,
        mixed_rows,
        branch,
        middle,
        normed_two,
        pre_act,
        active,
        mlp_out,
    ) = saved_set
    model_width = attn_full.shape[0]
    hidden = mlp_full.shape[1] // 2
    vec_rows = vectors_full.astype(jnp.float32)
    n_seq = lax.axis_size("seq")
    images, token_rows, _ = upstream.shape
    length = token_rows * n_seq
    group_width = model_width // n_seq
    per_group = group_width // HD
    grad_scale_two = jnp.sum(upstream * mlp_out, axis=(0, 1))
    grad_mlp_out = (upstream * vec_rows[9]).astype(jnp.bfloat16)
    grad_bias_down = jnp.sum(grad_mlp_out.astype(jnp.float32), axis=(0, 1))
    grad_down = contract_rows(grad_mlp_out, active)
    grad_active = jnp.dot(grad_mlp_out, mlp_full[:, hidden:], preferred_element_type=jnp.float32)
    _, gelu_pull = jax.vjp(gelu_exact, pre_act)
    grad_pre = gelu_pull(grad_active)[0].astype(jnp.bfloat16)
    grad_bias_up = jnp.sum(grad_pre.astype(jnp.float32), axis=(0, 1))
    grad_up = contract_rows(normed_two, grad_pre)
    grad_normed_two = contract_last(grad_pre, mlp_full[:, :hidden])
    _, second_pull = jax.vjp(layer_norm, middle, vec_rows[6], vec_rows[7])
    grad_mid_norm, grad_gain_two, grad_shift_two = second_pull(grad_normed_two)
    grad_middle = upstream + grad_mid_norm
    grad_scale_one = jnp.sum(grad_middle * branch, axis=(0, 1))
    grad_branch = (grad_middle * vec_rows[5]).astype(jnp.bfloat16)
    grad_bias_proj = jnp.sum(grad_branch.astype(jnp.float32), axis=(0, 1))
    grad_proj = contract_rows(grad_branch, mixed_rows)
    grad_mixed = jnp.dot(
        grad_branch, attn_full[:, 3 * model_width :], preferred_element_type=jnp.float32
    ).astype(jnp.bfloat16)
    grad_heads = lax.all_to_all(
        grad_mixed.reshape(images, token_rows, n_seq, group_width),
        "seq",
        split_axis=2,
        concat_axis=1,
        tiled=True,
    )
    grad_items = (
        grad_heads.reshape(images, length, per_group, HD)
        .transpose(0, 2, 1, 3)
        .reshape(images * per_group, length, HD)
    )
    grad_stack = lax.map(
        attend_back, (stacked[0], stacked[1], stacked[2], mask_heads, log_total, grad_items)
    )
    grad_stack = (
        grad_stack.reshape(images, per_group, 3, length, HD)
        .transpose(0, 3, 2, 1, 4)
        .reshape(images, length, 3, 1, group_width)
    )
    grad_qkv = lax.all_to_all(grad_stack, "seq", split_axis=1, concat_axis=3, tiled=True).reshape(
        images, token_rows, 3 * model_width
    )
    grad_qkv_sum = jnp.sum(grad_qkv.astype(jnp.float32), axis=(0, 1))
    grad_qkv_weight = contract_rows(normed, grad_qkv)
    grad_normed = contract_last(grad_qkv, attn_full[:, : 3 * model_width])
    _, first_pull = jax.vjp(layer_norm, inputs, vec_rows[0], vec_rows[1])
    grad_in_norm, grad_gain_one, grad_shift_one = first_pull(grad_normed)
    grad_inputs = grad_middle + grad_in_norm
    grad_attn = jnp.concatenate([grad_qkv_weight, grad_proj], axis=1)
    grad_mlp = jnp.concatenate([grad_up, grad_down], axis=1)
    grad_rows = jnp.stack(
        [
            grad_gain_one,
            grad_shift_one,
            grad_qkv_sum[:model_width],
            grad_qkv_sum[2 * model_width :],
            grad_bias_proj,
            grad_scale_one,
            grad_gain_two,
            grad_shift_two,
            grad_bias_down,
            grad_scale_two,
        ]
    )
    grad_vec = jnp.concatenate(
        [grad_rows, grad_bias_up.reshape(hidden // model_width, model_width)], axis=0
    )
    return (grad_inputs, (grad_attn, grad_mlp, grad_vec))


def adam_step(weights, gradient, moment_one, moment_two, step_rate, decay_weight):
    one_new = beta_first * moment_one + (1.0 - beta_first) * gradient
    two_new = beta_second * moment_two + (1.0 - beta_second) * gradient * gradient
    one_hat = one_new / (1.0 - beta_first**step_count)
    two_hat = two_new / (1.0 - beta_second**step_count)
    change = -step_rate * (
        one_hat / (jnp.sqrt(two_hat) + adam_eps) + decay_weight * weights.astype(jnp.float32)
    )
    return (change, one_new, two_new)


def local(
    tokens_in,
    key_mask,
    attn_weights,
    mlp_weights,
    vectors,
    cotangent,
    first_attn,
    second_attn,
    first_mlp,
    second_mlp,
    first_vec,
    second_vec,
):
    layers = attn_weights.shape[0]
    n_seq = lax.axis_size("seq")
    per_group = attn_weights.shape[2] // 4 // n_seq // HD
    mask_heads = jnp.repeat(key_mask, per_group, axis=0)
    residual = tokens_in.astype(jnp.float32)
    stored = []
    gathered_sets = []
    for layer_index in range(layers):
        weight_set = (
            lax.all_gather(attn_weights[layer_index], "fsdp", axis=0, tiled=True),
            lax.all_gather(mlp_weights[layer_index], "fsdp", axis=0, tiled=True),
            lax.all_gather(vectors[layer_index], "fsdp", axis=1, tiled=True),
        )
        residual, saved_set = forward_layer(
            residual, mask_heads, weight_set[0], weight_set[1], weight_set[2]
        )
        stored.append(saved_set)
        gathered_sets.append(weight_set)
    upstream = cotangent.astype(jnp.float32)
    layer_grads = [None] * layers
    for layer_index in reversed(range(layers)):
        weight_set = (
            lax.all_gather(attn_weights[layer_index], "fsdp", axis=0, tiled=True),
            lax.all_gather(mlp_weights[layer_index], "fsdp", axis=0, tiled=True),
            lax.all_gather(vectors[layer_index], "fsdp", axis=1, tiled=True),
        )
        upstream, local_grads = backward_layer(
            upstream, stored[layer_index], weight_set[0], weight_set[1], weight_set[2], mask_heads
        )
        owned = (
            lax.psum_scatter(
                local_grads[0].astype(jnp.bfloat16), "fsdp", scatter_dimension=0, tiled=True
            ).astype(jnp.float32),
            lax.psum_scatter(
                local_grads[1].astype(jnp.bfloat16), "fsdp", scatter_dimension=0, tiled=True
            ).astype(jnp.float32),
            lax.psum_scatter(
                local_grads[2].astype(jnp.bfloat16), "fsdp", scatter_dimension=1, tiled=True
            ).astype(jnp.float32),
        )
        owned = (
            lax.psum(owned[0].astype(jnp.bfloat16), ("dp", "seq")).astype(jnp.float32),
            lax.psum(owned[1].astype(jnp.bfloat16), ("dp", "seq")).astype(jnp.float32),
            lax.psum(owned[2].astype(jnp.bfloat16), ("dp", "seq")).astype(jnp.float32),
        )
        layer_grads[layer_index] = owned
    grad_attn = jnp.stack([layer_grads[index_one][0] for index_one in range(layers)])
    grad_mlp = jnp.stack([layer_grads[index_one][1] for index_one in range(layers)])
    grad_vectors = jnp.stack([layer_grads[index_one][2] for index_one in range(layers)])
    step_attn, one_attn, two_attn = adam_step(
        attn_weights, grad_attn, first_attn, second_attn, rate_matrix, decay_rate
    )
    step_mlp, one_mlp, two_mlp = adam_step(
        mlp_weights, grad_mlp, first_mlp, second_mlp, rate_matrix, decay_rate
    )
    step_vectors, one_vec, two_vec = adam_step(
        vectors, grad_vectors, first_vec, second_vec, rate_vector, 0.0
    )
    return (
        residual,
        upstream,
        grad_attn,
        grad_mlp,
        grad_vectors,
        step_attn,
        step_mlp,
        step_vectors,
        one_attn,
        two_attn,
        one_mlp,
        two_mlp,
        one_vec,
        two_vec,
    )


def solution(mesh):
    return jax.shard_map(
        local,
        mesh=mesh,
        in_specs=(
            P(("dp", "fsdp"), "seq", None),
            P(("dp", "fsdp"), None),
            P(None, "fsdp", None),
            P(None, "fsdp", None),
            P(None, None, "fsdp"),
            P(("dp", "fsdp"), "seq", None),
            P(None, "fsdp", None),
            P(None, "fsdp", None),
            P(None, "fsdp", None),
            P(None, "fsdp", None),
            P(None, None, "fsdp"),
            P(None, None, "fsdp"),
        ),
        out_specs=(
            P(("dp", "fsdp"), "seq", None),
            P(("dp", "fsdp"), "seq", None),
            P(None, "fsdp", None),
            P(None, "fsdp", None),
            P(None, None, "fsdp"),
            P(None, "fsdp", None),
            P(None, "fsdp", None),
            P(None, None, "fsdp"),
            P(None, "fsdp", None),
            P(None, "fsdp", None),
            P(None, "fsdp", None),
            P(None, "fsdp", None),
            P(None, None, "fsdp"),
            P(None, None, "fsdp"),
        ),
        check_vma=False,
    )
```

profile of v0, /device:TPU:0, one launch (start us, length us, event | category | flops | bytes accessed | tf_op | source)
XLA Modules:
  0.0 2304.5 jit_solution(1958127319763447503)
XLA Ops:
  16.5 23.2 %all-gather = bf16[1,14,1024]{2,0,1:T(2,128)(2,1)S(1)} all-gather(bf16[1,14,128]{2,0,1:T(2,128)(2,1)S(1)} %get-tuple-element.468), channel_id=2, replica_groups=mesh['dp'=2,'fsdp'=8,'seq'=2] {'fsdp'}, dimensions={2}, use_global_device_ids=true | all-gather | bytes 32256 | tf_op jit(solution)/shard_map/all_gather | solution.py:273
  39.9 17.4 all-gather.3
  59.9 79.7 %all-gather.11.cloned.1.call-done = bf16[1,1024,4096]{2,1,0:T(8,128)(2,1)} async-done(((bf16[1,128,4096]{2,1,0:T(8,128)(2,1)}), bf16[1,1024,4096]{2,1,0:T(8,128)(2,1)}) %all-gather.11.cloned.1.call-update) | async-done | bytes 8388624 | tf_op jit(solution)/shard_map/all_gather | solution.py:271
  166.1 10.3 copy.103
  198.8 72.4 %while.44 = (s32[]{:T(128)}, bf16[8,1040,64]{1,2,0:T(8,128)(2,1)}, f32[8,1040]{1,0:T(8,128)S(1)}, s32[8,1040]{1,0:T(8,128)S(1)}, bf16[8,1040,64]{2,1,0:T(8,128)(...) while((s32[]{:T(128)}, bf16[8,1040,64]{1,2,0:T(8,128)(2,1)}, ...), condition=%wide.region_5.6_spmd, body=%wide.region_2.5_spmd.sunk | while | flops 285608960 | bytes 31756240 | solution.py:110
  305.0 63.0 %all-gather.13.cloned.1.call-done = bf16[1,1024,8192]{2,1,0:T(8,128)(2,1)} async-done(((bf16[1,128,8192]{2,1,0:T(8,128)(2,1)}), bf16[1,1024,8192]{2,1,0:T(8,128)(2,1)}) %all-gather.13.cloned.1.call-update) | async-done | bytes 16777232 | tf_op jit(solution)/shard_map/all_gather | solution.py:272
  368.1 27.1 %multiply_convert_fusion.3 = (bf16[520,4096]{1,0:T(8,128)(2,1)S(1)}, f32[520,4096]{1,0:T(8,128)}, f32[520,4096]{1,0:T(8,128)}) fusion(f32[4096]{0:T(1024)S(1)} %bitcast.487, bf16[1024,8192]{1,0:T(8,128)(2,1)} %bitcast.522, f32[1,520,1024]{2,1,0:T(8,128)S(1)} %get-tuple-element.424, f32[1024]{0:T(1024)S(1)} %bitcast.513, f32[1024]{0:T(1024)S(1)} %bitcast.499, ...), kind=kOutput, calls=%fused_computation.138 | convolution fusion | flops 4505313280 | bytes 31846464 | tf_op jit(solution)/shard_map/dot_general | solution.py:122
  395.3 11.5 fusion.224
  407.2 86.7 %all-gather.15.cloned.1.call-done = bf16[1,1024,4096]{2,1,0:T(8,128)(2,1)} async-done(((bf16[1,128,4096]{2,1,0:T(8,128)(2,1)}), bf16[1,1024,4096]{2,1,0:T(8,128)(2,1)}) %all-gather.15.cloned.1.call-update) | async-done | bytes 8388624 | tf_op jit(solution)/shard_map/all_gather | solution.py:271
  520.5 10.3 copy.110
  552.9 68.8 %while.45 = (s32[]{:T(128)}, bf16[8,1040,64]{1,2,0:T(8,128)(2,1)S(1)}, f32[8,1040]{1,0:T(8,128)S(1)}, s32[8,1040]{1,0:T(8,128)S(1)}, bf16[8,1040,64]{2,1,0:T(8,1...) while((s32[]{:T(128)}, ...), condition=%wide.region_13.14_spmd, body=%wide.region_10.13_spmd.sunk | while | flops 285608960 | bytes 31763296 | solution.py:110
  654.4 67.8 %all-gather.17.cloned.1.call-done = bf16[1,1024,8192]{2,1,0:T(8,128)(2,1)} async-done(((bf16[1,128,8192]{2,1,0:T(8,128)(2,1)}), bf16[1,1024,8192]{2,1,0:T(8,128)(2,1)}) %all-gather.17.cloned.1.call-update) | async-done | bytes 16777232 | tf_op jit(solution)/shard_map/all_gather | solution.py:272
  722.3 28.0 %multiply_convert_fusion.2 = (bf16[520,4096]{1,0:T(8,128)(2,1)}, f32[520,4096]{1,0:T(8,128)}, f32[520,4096]{1,0:T(8,128)}) fusion(f32[4096]{0:T(1024)S(1)} %bitcast.489, bf16[1024,8192]{1,0:T(8,128)(2,1)} %bitcast.526, f32[1,520,1024]{2,1,0:T(8,128)} %copy-done.8, f32[1024]{0:T(1024)S(1)} %bitcast.511, f32[1024]{0:T(1024)S(1)} %bitcast.495, ...), kind=kOutput, calls=%fused_computation.125 | convolution fusion | flops 4505313280 | bytes 31846464 | tf_op jit(solution)/shard_map/dot_general | solution.py:122
  750.4 14.5 fusion.234
  764.9 9.6 fusion.153
  792.1 99.1 %while.46 = (s32[]{:T(128)}, bf16[8,3,1040,64]{2,3,1,0:T(8,128)(2,1)S(1)}, s32[8,1040]{1,0:T(8,128)}, bf16[8,1040,64]{2,1,0:T(8,128)(2,1)}, bf16[8,1040,64]{2,1,...) while((s32[]{:T(128)}, ...), condition=%wide.region_20.21_spmd, body=%wide.region_18.20_spmd.sunk | while | flops 703489280 | bytes 35388936 | solution.py:198
  937.0 14.5 fusion.152
  952.4 14.3 fusion.235
  966.7 10.0 fusion.157
  997.4 99.1 %while.47 = (s32[]{:T(128)}, bf16[8,3,1040,64]{2,3,1,0:T(8,128)(2,1)S(1)}, s32[8,1040]{1,0:T(8,128)}, bf16[8,1040,64]{2,1,0:T(8,128)(2,1)}, bf16[8,1040,64]{2,1,...) while((s32[]{:T(128)}, ...), condition=%wide.region_27.28_spmd, body=%wide.region_25.27_spmd.sunk | while | flops 703489280 | bytes 35388936 | solution.py:198
  1130.9 9.4 convolution_convert_fusion.5
  1177.0 9.6 convolution_convert_fusion.3
  1203.3 9.6 convolution_convert_fusion.1
  1237.8 56.8 %reduce-scatter.11.cloned.1.call-done = bf16[128,4096]{1,0:T(8,128)(2,1)} async-done(((bf16[1024,4096]{1,0:T(8,128)(2,1)}), bf16[128,4096]{1,0:T(8,128)(2,1)}) %reduce-scatter.11.cloned.1.call-update) | async-done | bytes 1048592 | tf_op jit(solution)/shard_map/reduce_scatter | solution.py:292
  1294.7 152.5 %reduce-scatter.13.cloned.1.call-done = bf16[128,4096]{1,0:T(8,128)(2,1)} async-done(((bf16[1024,4096]{1,0:T(8,128)(2,1)}), bf16[128,4096]{1,0:T(8,128)(2,1)}) %reduce-scatter.13.cloned.1.call-update) | async-done | bytes 1048592 | tf_op jit(solution)/shard_map/reduce_scatter | solution.py:292
  1447.2 285.6 %reduce-scatter.15.cloned.1.call-done = bf16[128,8192]{1,0:T(8,128)(2,1)} async-done(((bf16[1024,8192]{1,0:T(8,128)(2,1)}), bf16[128,8192]{1,0:T(8,128)(2,1)}) %reduce-scatter.15.cloned.1.call-update) | async-done | bytes 2097168 | tf_op jit(solution)/shard_map/reduce_scatter | solution.py:295
  1732.8 286.1 %reduce-scatter.17.cloned.1.call-done = bf16[128,8192]{1,0:T(8,128)(2,1)} async-done(((bf16[1024,8192]{1,0:T(8,128)(2,1)}), bf16[128,8192]{1,0:T(8,128)(2,1)}) %reduce-scatter.17.cloned.1.call-update) | async-done | bytes 2097168 | tf_op jit(solution)/shard_map/reduce_scatter | solution.py:295
  2022.6 60.4 %reduce-scatter.19.cloned.1.call-done = bf16[128,14]{1,0:T(8,128)(2,1)} async-done(((bf16[1024,14]{1,0:T(8,128)(2,1)}), bf16[128,14]{1,0:T(8,128)(2,1)}) %reduce-scatter.19.cloned.1.call-update) | async-done | bytes 3600
  2083.9 63.2 %reduce-scatter.21.cloned.1.call-done = bf16[128,14]{1,0:T(8,128)(2,1)} async-done(((bf16[1024,14]{1,0:T(8,128)(2,1)}), bf16[128,14]{1,0:T(8,128)(2,1)}) %reduce-scatter.21.cloned.1.call-update) | async-done | bytes 3600
  2156.2 112.7 %all-reduce.4.cloned.1.call-done = (bf16[1,128,4096]{2,1,0:T(8,128)(2,1)}, bf16[1,128,4096]{2,1,0:T(8,128)(2,1)}, bf16[1,128,8192]{2,1,0:T(8,128)(2,1)}, bf16[1,128,8192]{2,1,0:T(8,128)(2,1)}) async-done(((bf16[1,128,4096]{2,1,0:T(8,128)(2,1)}, bf16[1,128,4096]{2,1,0:T(8,128)(2,1)}, bf16[1,128,8192]{2,1,0:T(8,128)(2,1)}, bf16[1,128,8192]{2,1,0:T(8,128)(2,1)}), (bf16[1,128,4096]{2,1,0:T(8,128)(2,1)}, ...) | async-done | bytes 6291472 | tf_op jit(solution)/shard_map/psum | solution.py:303
  2268.9 19.0 add_multiply_fusion
  2288.0 9.8 add_multiply_fusion.1
  (712 shorter events, 724.4 us)
Async XLA Ops:
  7.2 132.3 %all-gather.11.cloned.1.call-start = ((), (), s32[]{:S(2)}) async-start(), calls=%async_computation.18 | async-start | bytes 9437184 | tf_op jit(solution)/shard_map/all_gather | solution.py:271
  10.3 357.7 %all-gather.13.cloned.1.call-start = ((), (), s32[]{:S(2)}) async-start(), calls=%async_computation.19 | async-start | bytes 18874368 | tf_op jit(solution)/shard_map/all_gather | solution.py:272
  15.1 478.8 %all-gather.15.cloned.1.call-start = ((), (), s32[]{:S(2)}) async-start(), calls=%async_computation.20 | async-start | bytes 9437184 | tf_op jit(solution)/shard_map/all_gather | solution.py:271
  15.8 706.5 %all-gather.17.cloned.1.call-start = ((), (), s32[]{:S(2)}) async-start(), calls=%async_computation.21 | async-start | bytes 18874368 | tf_op jit(solution)/shard_map/all_gather | solution.py:272
  16.4 1278.3 %reduce-scatter.11.cloned.1.call-start = ((), (), s32[]{:S(2)}) async-start(), calls=%async_computation.14 | async-start | bytes 9437184 | tf_op jit(solution)/shard_map/reduce_scatter | solution.py:292
  39.7 107.9 %copy-start.49 = (f32[1,1,1024]{2,0,1:T(1,128)}, f32[1,1,1024]{2,0,1:T(1,128)S(1)}, u32[]{:S(2)}) copy-start(f32[1,1,1024]{2,0,1:T(1,128)S(1)} %get-tuple-element.463) | copy-start | bytes 12292
  39.8 107.8 %copy-start.106 = (f32[1,1,1024]{2,0,1:T(1,128)}, f32[1,1,1024]{2,0,1:T(1,128)S(1)}, u32[]{:S(2)}) copy-start(f32[1,1,1024]{2,0,1:T(1,128)S(1)} %get-tuple-element.464) | copy-start | bytes 12292
  39.8 260.1 %copy-start.66 = (f32[1,1,1024]{2,0,1:T(1,128)}, f32[1,1,1024]{2,0,1:T(1,128)S(1)}, u32[]{:S(2)}) copy-start(f32[1,1,1024]{2,0,1:T(1,128)S(1)} %get-tuple-element.461) | copy-start | bytes 12292
  39.8 260.1 %copy-start.68 = (f32[1,1,1024]{2,0,1:T(1,128)}, f32[1,1,1024]{2,0,1:T(1,128)S(1)}, u32[]{:S(2)}) copy-start(f32[1,1,1024]{2,0,1:T(1,128)S(1)} %get-tuple-element.462) | copy-start | bytes 12292
  39.8 328.3 %copy-start.77 = (f32[1,1,1024]{2,0,1:T(1,128)}, f32[1,1,1024]{2,0,1:T(1,128)S(1)}, u32[]{:S(2)}) copy-start(f32[1,1,1024]{2,0,1:T(1,128)S(1)} %get-tuple-element.459) | copy-start | bytes 12292
  39.8 328.3 %copy-start.104 = (f32[1,1,1024]{2,0,1:T(1,128)}, f32[1,1,1024]{2,0,1:T(1,128)S(1)}, u32[]{:S(2)}) copy-start(f32[1,1,1024]{2,0,1:T(1,128)S(1)} %get-tuple-element.460) | copy-start | bytes 12292
  39.8 355.4 %copy-start.70 = (f32[1,1,1024]{2,0,1:T(1,128)}, f32[1,1,1024]{2,0,1:T(1,128)S(1)}, u32[]{:S(2)}) copy-start(f32[1,1,1024]{2,0,1:T(1,128)S(1)} %get-tuple-element.457) | copy-start | bytes 12292
  39.8 355.4 %copy-start.110 = (f32[1,1,1024]{2,0,1:T(1,128)}, f32[1,1,1024]{2,0,1:T(1,128)S(1)}, u32[]{:S(2)}) copy-start(f32[1,1,1024]{2,0,1:T(1,128)S(1)} %get-tuple-element.458) | copy-start | bytes 12292
  39.9 328.2 %copy-start.72 = (f32[1,4,1024]{2,0,1:T(1,128)}, f32[1,4,1024]{2,0,1:T(1,128)S(1)}, u32[]{:S(2)}) copy-start(f32[1,4,1024]{2,0,1:T(1,128)S(1)} %slice.263) | copy-start | bytes 49156
  395.3 98.6 %copy-start.81 = (f32[1,1,1024]{2,0,1:T(1,128)S(1)}, f32[1,1,1024]{2,0,1:T(1,128)}, u32[]{:S(2)}) copy-start(f32[1,1,1024]{2,0,1:T(1,128)} %get-tuple-element.453) | copy-start | bytes 12292
  395.3 98.6 %copy-start.93 = (f32[3072]{0:T(1024)S(1)}, f32[3072]{0:T(1024)}, u32[]{:S(2)}) copy-start(f32[3072]{0:T(1024)} %get-tuple-element.473) | copy-start | bytes 36868
  395.3 98.6 %copy-start.108 = (f32[1,1,1024]{2,0,1:T(1,128)S(1)}, f32[1,1,1024]{2,0,1:T(1,128)}, u32[]{:S(2)}) copy-start(f32[1,1,1024]{2,0,1:T(1,128)} %get-tuple-element.454) | copy-start | bytes 12292
  406.8 240.9 %copy-start.5 = (f32[1,520,1024]{2,1,0:T(8,128)}, f32[1,520,1024]{2,1,0:T(8,128)S(1)}, u32[]{:S(2)}) copy-start(f32[1,520,1024]{2,1,0:T(8,128)S(1)} %get-tuple-element.420) | copy-start | bytes 6389764
  406.8 95.1 %copy-start.59 = (f32[520]{0:T(1024)}, f32[520]{0:T(1024)S(1)}, u32[]{:S(2)}) copy-start(f32[520]{0:T(1024)S(1)} %broadcast_multiply_fusion.1) | copy-start | bytes 6244
  652.6 122.0 %copy-start.62 = (f32[520]{0:T(1024)}, f32[520]{0:T(1024)S(1)}, u32[]{:S(2)}) copy-start(f32[520]{0:T(1024)S(1)} %broadcast_multiply_fusion) | copy-start | bytes 6244
  654.4 120.1 %copy-start.89 = (f32[520]{0:T(1024)}, f32[520]{0:T(1024)S(1)}, u32[]{:S(2)}) copy-start(f32[520]{0:T(1024)S(1)} %fusion.202) | copy-start | bytes 6244
  1147.4 299.8 %reduce-scatter.13.cloned.1.call-start = ((), (), s32[]{:S(2)}) async-start(), calls=%async_computation.15 | async-start | bytes 9437184 | tf_op jit(solution)/shard_map/reduce_scatter | solution.py:292
  1167.9 564.9 %reduce-scatter.15.cloned.1.call-start = ((), (), s32[]{:S(2)}) async-start(), calls=%async_computation.16 | async-start | bytes 18874368 | tf_op jit(solution)/shard_map/reduce_scatter | solution.py:295
  1193.3 825.6 %reduce-scatter.17.cloned.1.call-start = ((), (), s32[]{:S(2)}) async-start(), calls=%async_computation.17 | async-start | bytes 18874368 | tf_op jit(solution)/shard_map/reduce_scatter | solution.py:295
  1219.5 863.6 %reduce-scatter.19.cloned.1.call-start = ((), (), s32[]{:S(2)}) async-start(), calls=%async_computation.22 | async-start | bytes 294912
  1234.0 913.1 %reduce-scatter.21.cloned.1.call-start = ((), (), s32[]{:S(2)}) async-start(), calls=%async_computation.23 | async-start | bytes 294912
  1237.6 781.4 %copy-start.13 = (f32[520,1024]{1,0:T(8,128)S(1)}, f32[520,1024]{1,0:T(8,128)}, u32[]{:S(2)}) copy-start(f32[520,1024]{1,0:T(8,128)} %copy-done.12) | copy-start | bytes 6389764
  1237.6 781.4 %copy-start.18 = (bf16[1,520,1024]{2,1,0:T(8,128)(2,1)S(1)}, bf16[1,520,1024]{2,1,0:T(8,128)(2,1)}, u32[]{:S(2)}) copy-start(bf16[1,520,1024]{2,1,0:T(8,128)(2,1)} %param.20) | copy-start | bytes 3194884
  1237.6 1031.3 %all-reduce.4.cloned.1.call-start = ((), (), s32[]{:S(2)}) async-start(), calls=%async_computation.24 | async-start | bytes 12582912 | tf_op jit(solution)/shard_map/psum | solution.py:303
  2019.0 134.8 %copy-start.47 = (bf16[2,14,128]{2,0,1:T(2,128)(2,1)S(1)}, bf16[2,14,128]{2,0,1:T(2,128)(2,1)}, u32[]{:S(2)}) copy-start(bf16[2,14,128]{2,0,1:T(2,128)(2,1)} %param.24) | copy-start | bytes 21508
  2019.0 134.8 %copy-start.91 = (f32[2,14,128]{2,0,1:T(2,128)S(1)}, f32[2,14,128]{2,0,1:T(2,128)}, u32[]{:S(2)}) copy-start(f32[2,14,128]{2,0,1:T(2,128)} %param.30) | copy-start | bytes 43012
  2019.0 134.8 %copy-start.92 = (f32[2,14,128]{2,0,1:T(2,128)S(1)}, f32[2,14,128]{2,0,1:T(2,128)}, u32[]{:S(2)}) copy-start(f32[2,14,128]{2,0,1:T(2,128)} %param.31) | copy-start | bytes 43012
  (115 other events, 1775.4 us)
Sparse Core Ops, SparseCore 0:
  10.7 128.7 all-gather.10
  142.2 225.7 all-gather.12
  370.8 123.1 all-gather.14
  496.5 225.7 all-gather.16
  1147.5 147.1 reduce-scatter.10
  1299.2 147.9 reduce-scatter.12
  1451.0 281.8 reduce-scatter.14
  1737.1 281.7 reduce-scatter.16
  2022.8 60.2 reduce-scatter.18
  2086.8 60.2 reduce-scatter.20
  2149.7 119.1 all-reduce.3
where the time goes:
time: 2320 us; the launch traced here: 2300 us
  waiting for transfers between devices  1320 us (57%)
  matrix products  486 us (21%)
  local copies, waits for them, and re-layouts  247 us (11%)
  other arithmetic  136 us (6%)
  blocking collectives  101 us (4%)
    reduce_scatter x2, waiting for transfers between devices, local(): lax.psum_scatter(local_grads[1].astype(jnp.bfloat16), 'fsdp', scatter_dim...  572 us
    reduce_scatter x2, waiting for transfers between devices, local(): lax.psum_scatter(local_grads[0].astype(jnp.bfloat16), 'fsdp', scatter_dim...  209 us
    dot_general x56, matrix products, contract_last(): lax.dot_general(left_side, right_side, (((left_side.ndim - 1,), (1,)), ((...  176 us
    all_gather x2, waiting for transfers between devices, local(): lax.all_gather(attn_weights[layer_index], 'fsdp', axis=0, tiled=True)  166 us
    all_gather x2, waiting for transfers between devices, local(): lax.all_gather(mlp_weights[layer_index], 'fsdp', axis=0, tiled=True)  131 us
    unnamed x13, waiting for transfers between devices  125 us
    psum x1, waiting for transfers between devices, local(): lax.psum(owned[0].astype(jnp.bfloat16), ('dp', 'seq')).astype(jnp.float32)  113 us
    dot_general x8, matrix products, contract_rows(): lax.dot_general(left_side, right_side, (((0, 1), (0, 1)), ((), ())), pref...  62.7 us
  transfers between devices with their start and end apart: 11, of which 11 were waited for; matrix products, arithmetic and copies ran while one was open for 17% of the time, Pallas kernels for 0%

commit v1 on v0

--- a/solution.py
+++ b/solution.py
@@ -13,6 +13,11 @@
 rate_matrix = 0.01
 rate_vector = 0.05
 step_count = 10.0
+
+
+def one_after_other(value, inner_axis, outer_axis):
+    inner = lax.psum(value, inner_axis)
+    return lax.psum(inner, outer_axis)
 
 
 def layer_norm(values, norm_gain, norm_shift):
@@ -300,7 +305,7 @@
             ).astype(jnp.float32),
         )
         owned = (
-            lax.psum(owned[0].astype(jnp.bfloat16), ("dp", "seq")).astype(jnp.float32),
+            one_after_other(owned[0].astype(jnp.bfloat16), "dp", "seq").astype(jnp.float32),
             lax.psum(owned[1].astype(jnp.bfloat16), ("dp", "seq")).astype(jnp.float32),
             lax.psum(owned[2].astype(jnp.bfloat16), ("dp", "seq")).astype(jnp.float32),
         )

time: 2320 us -> 2360 us (1.017)
  waiting for transfers between devices: 1320 us -> 1360 us
    reduce_scatter x2, waiting for transfers between devices: 209 us -> 266 us  [local(): lax.psum_scatter(local_grads[0].astype(jnp.bfloat16), 'fsdp', scatter_dim...]
    psum x1 -> x3, waiting for transfers between devices: 113 us -> 96.9 us  [the longest x1 78.9 us: local(): lax.psum(owned[1].astype(jnp.bfloat16), ('dp', 'seq')).astype(jnp.float32)]
    unnamed x13 -> x15, waiting for transfers between devices: 125 us -> 126 us
  transfers between devices with their start and end apart: 11 -> 13, of which waited for: 11 -> 13; matrix products, arithmetic and copies ran while one was open for 17% -> 18% of each run, Pallas kernels for 0% -> 0%
where the time goes in v1:
time: 2360 us; the launch traced here: 2350 us
  waiting for transfers between devices  1360 us (58%)
  matrix products  488 us (21%)
  local copies, waits for them, and re-layouts  249 us (11%)
  other arithmetic  136 us (6%)
  blocking collectives  101 us (4%)
    reduce_scatter x2, waiting for transfers between devices, local(): lax.psum_scatter(local_grads[1].astype(jnp.bfloat16), 'fsdp', scatter_dim...  572 us
    reduce_scatter x2, waiting for transfers between devices, local(): lax.psum_scatter(local_grads[0].astype(jnp.bfloat16), 'fsdp', scatter_dim...  266 us
    dot_general x56, matrix products, contract_last(): lax.dot_general(left_side, right_side, (((left_side.ndim - 1,), (1,)), ((...  176 us
    all_gather x2, waiting for transfers between devices, local(): lax.all_gather(attn_weights[layer_index], 'fsdp', axis=0, tiled=True)  166 us
    all_gather x2, waiting for transfers between devices, local(): lax.all_gather(mlp_weights[layer_index], 'fsdp', axis=0, tiled=True)  131 us
    unnamed x15, waiting for transfers between devices  126 us
    psum x1, waiting for transfers between devices, local(): lax.psum(owned[1].astype(jnp.bfloat16), ('dp', 'seq')).astype(jnp.float32)  78.9 us
    dot_general x8, matrix products, contract_rows(): lax.dot_general(left_side, right_side, (((0, 1), (0, 1)), ((), ())), pref...  64.7 us
  transfers between devices with their start and end apart: 13, of which 13 were waited for; matrix products, arithmetic and copies ran while one was open for 18% of the time, Pallas kernels for 0%

profile of v1, /device:TPU:0, one launch (start us, length us, event | category | flops | bytes accessed | tf_op | source)
XLA Modules:
  0.0 2350.7 jit_solution(13678598487474144911)
XLA Ops:
  16.5 23.2 all-gather
  39.9 17.4 all-gather.3
  59.9 79.7 %all-gather.11.cloned.1.call-done = bf16[1,1024,4096]{2,1,0:T(8,128)(2,1)} async-done(((bf16[1,128,4096]{2,1,0:T(8,128)(2,1)}), bf16[1,1024,4096]{2,1,0:T(8,128)(2,1)}) %all-gather.11.cloned.1.call-update) | async-done | bytes 8388624 | tf_op jit(solution)/shard_map/all_gather | solution.py:276
  166.1 10.3 copy.103
  198.8 72.4 %while.44 = (s32[]{:T(128)}, bf16[8,1040,64]{1,2,0:T(8,128)(2,1)}, f32[8,1040]{1,0:T(8,128)S(1)}, s32[8,1040]{1,0:T(8,128)S(1)}, bf16[8,1040,64]{2,1,0:T(8,128)(...) while((s32[]{:T(128)}, bf16[8,1040,64]{1,2,0:T(8,128)(2,1)}, ...), condition=%wide.region_5.6_spmd, body=%wide.region_2.5_spmd.sunk | while | flops 285608960 | bytes 31756240 | solution.py:115
  305.1 63.0 %all-gather.13.cloned.1.call-done = bf16[1,1024,8192]{2,1,0:T(8,128)(2,1)} async-done(((bf16[1,128,8192]{2,1,0:T(8,128)(2,1)}), bf16[1,1024,8192]{2,1,0:T(8,128)(2,1)}) %all-gather.13.cloned.1.call-update) | async-done | bytes 16777232 | tf_op jit(solution)/shard_map/all_gather | solution.py:277
  368.1 27.0 %multiply_convert_fusion.3 = (bf16[520,4096]{1,0:T(8,128)(2,1)S(1)}, f32[520,4096]{1,0:T(8,128)}, f32[520,4096]{1,0:T(8,128)}) fusion(f32[4096]{0:T(1024)S(1)} %bitcast.487, bf16[1024,8192]{1,0:T(8,128)(2,1)} %bitcast.522, f32[1,520,1024]{2,1,0:T(8,128)S(1)} %get-tuple-element.426, f32[1024]{0:T(1024)S(1)} %bitcast.513, f32[1024]{0:T(1024)S(1)} %bitcast.503, ...), kind=kOutput, calls=%fused_computation.138 | convolution fusion | flops 4505313280 | bytes 31846464 | tf_op jit(solution)/shard_map/dot_general | solution.py:127
  395.2 11.5 fusion.224
  407.2 86.8 %all-gather.15.cloned.1.call-done = bf16[1,1024,4096]{2,1,0:T(8,128)(2,1)} async-done(((bf16[1,128,4096]{2,1,0:T(8,128)(2,1)}), bf16[1,1024,4096]{2,1,0:T(8,128)(2,1)}) %all-gather.15.cloned.1.call-update) | async-done | bytes 8388624 | tf_op jit(solution)/shard_map/all_gather | solution.py:276
  520.5 10.2 copy.110
  552.9 68.8 %while.45 = (s32[]{:T(128)}, bf16[8,1040,64]{1,2,0:T(8,128)(2,1)S(1)}, f32[8,1040]{1,0:T(8,128)S(1)}, s32[8,1040]{1,0:T(8,128)S(1)}, bf16[8,1040,64]{2,1,0:T(8,1...) while((s32[]{:T(128)}, ...), condition=%wide.region_13.14_spmd, body=%wide.region_10.13_spmd.sunk | while | flops 285608960 | bytes 31763296 | solution.py:115
  654.4 67.9 %all-gather.17.cloned.1.call-done = bf16[1,1024,8192]{2,1,0:T(8,128)(2,1)} async-done(((bf16[1,128,8192]{2,1,0:T(8,128)(2,1)}), bf16[1,1024,8192]{2,1,0:T(8,128)(2,1)}) %all-gather.17.cloned.1.call-update) | async-done | bytes 16777232 | tf_op jit(solution)/shard_map/all_gather | solution.py:277
  722.3 28.0 %multiply_convert_fusion.2 = (bf16[520,4096]{1,0:T(8,128)(2,1)}, f32[520,4096]{1,0:T(8,128)}, f32[520,4096]{1,0:T(8,128)}) fusion(f32[4096]{0:T(1024)S(1)} %bitcast.489, bf16[1024,8192]{1,0:T(8,128)(2,1)} %bitcast.526, f32[1,520,1024]{2,1,0:T(8,128)} %copy-done.8, f32[1024]{0:T(1024)S(1)} %bitcast.511, f32[1024]{0:T(1024)S(1)} %bitcast.495, ...), kind=kOutput, calls=%fused_computation.125 | convolution fusion | flops 4505313280 | bytes 31846464 | tf_op jit(solution)/shard_map/dot_general | solution.py:127
  750.4 14.5 fusion.234
  764.9 9.6 fusion.153
  792.1 99.1 %while.46 = (s32[]{:T(128)}, bf16[8,3,1040,64]{2,3,1,0:T(8,128)(2,1)S(1)}, s32[8,1040]{1,0:T(8,128)}, bf16[8,1040,64]{2,1,0:T(8,128)(2,1)}, bf16[8,1040,64]{2,1,...) while((s32[]{:T(128)}, ...), condition=%wide.region_20.21_spmd, body=%wide.region_18.20_spmd.sunk | while | flops 703489280 | bytes 35388936 | solution.py:203
  937.0 14.5 fusion.152
  952.4 14.3 fusion.235
  966.8 10.0 fusion.157
  997.2 99.1 %while.47 = (s32[]{:T(128)}, bf16[8,3,1040,64]{2,3,1,0:T(8,128)(2,1)S(1)}, s32[8,1040]{1,0:T(8,128)}, bf16[8,1040,64]{2,1,0:T(8,128)(2,1)}, bf16[8,1040,64]{2,1,...) while((s32[]{:T(128)}, ...), condition=%wide.region_27.28_spmd, body=%wide.region_25.27_spmd.sunk | while | flops 703489280 | bytes 35388936 | solution.py:203
  1169.3 11.6 convolution_convert_fusion.3
  1180.8 113.6 %reduce-scatter.11.cloned.1.call-done = bf16[128,4096]{1,0:T(8,128)(2,1)} async-done(((bf16[1024,4096]{1,0:T(8,128)(2,1)}), bf16[128,4096]{1,0:T(8,128)(2,1)}) %reduce-scatter.11.cloned.1.call-update) | async-done | bytes 1048592 | tf_op jit(solution)/shard_map/reduce_scatter | solution.py:297
  1294.5 152.5 %reduce-scatter.13.cloned.1.call-done = bf16[128,4096]{1,0:T(8,128)(2,1)} async-done(((bf16[1024,4096]{1,0:T(8,128)(2,1)}), bf16[128,4096]{1,0:T(8,128)(2,1)}) %reduce-scatter.13.cloned.1.call-update) | async-done | bytes 1048592 | tf_op jit(solution)/shard_map/reduce_scatter | solution.py:297
  1472.8 9.6 convolution_convert_fusion.1
  1511.7 286.7 %reduce-scatter.15.cloned.1.call-done = bf16[128,8192]{1,0:T(8,128)(2,1)} async-done(((bf16[1024,8192]{1,0:T(8,128)(2,1)}), bf16[128,8192]{1,0:T(8,128)(2,1)}) %reduce-scatter.15.cloned.1.call-update) | async-done | bytes 2097168 | tf_op jit(solution)/shard_map/reduce_scatter | solution.py:300
  1798.4 285.6 %reduce-scatter.17.cloned.1.call-done = bf16[128,8192]{1,0:T(8,128)(2,1)} async-done(((bf16[1024,8192]{1,0:T(8,128)(2,1)}), bf16[128,8192]{1,0:T(8,128)(2,1)}) %reduce-scatter.17.cloned.1.call-update) | async-done | bytes 2097168 | tf_op jit(solution)/shard_map/reduce_scatter | solution.py:300
  2087.7 60.7 %reduce-scatter.19.cloned.1.call-done = bf16[128,14]{1,0:T(8,128)(2,1)} async-done(((bf16[1024,14]{1,0:T(8,128)(2,1)}), bf16[128,14]{1,0:T(8,128)(2,1)}) %reduce-scatter.19.cloned.1.call-update) | async-done | bytes 3600
  2149.3 63.8 %reduce-scatter.21.cloned.1.call-done = bf16[128,14]{1,0:T(8,128)(2,1)} async-done(((bf16[1024,14]{1,0:T(8,128)(2,1)}), bf16[128,14]{1,0:T(8,128)(2,1)}) %reduce-scatter.21.cloned.1.call-update) | async-done | bytes 3600
  2222.2 13.6 all-reduce.10.cloned.1.call-done
  2235.8 10.4 add_multiply_fusion.1
  2246.2 78.9 %all-reduce.8.cloned.1.call-done = (bf16[1,128,8192]{2,1,0:T(8,128)(2,1)}, bf16[1,128,8192]{2,1,0:T(8,128)(2,1)}) async-done(((bf16[1,128,8192]{2,1,0:T(8,128)(2,1)}, bf16[1,128,8192]{2,1,0:T(8,128)(2,1)}), (bf16[1,128,8192]{2,1,0:T(8,128)(2,1)}, bf16[1,128,8192]{2,1,0:T(8,128)(2,1)})) %all-reduce.8.cloned.1.call-update) | async-done | bytes 4194320 | tf_op jit(solution)/shard_map/psum | solution.py:309
  2325.1 18.9 add_multiply_fusion
  (716 shorter events, 739.6 us)
Async XLA Ops:
  7.2 132.3 %all-gather.11.cloned.1.call-start = ((), (), s32[]{:S(2)}) async-start(), calls=%async_computation.18 | async-start | bytes 9437184 | tf_op jit(solution)/shard_map/all_gather | solution.py:276
  10.3 357.7 %all-gather.13.cloned.1.call-start = ((), (), s32[]{:S(2)}) async-start(), calls=%async_computation.19 | async-start | bytes 18874368 | tf_op jit(solution)/shard_map/all_gather | solution.py:277
  15.1 478.8 %all-gather.15.cloned.1.call-start = ((), (), s32[]{:S(2)}) async-start(), calls=%async_computation.20 | async-start | bytes 9437184 | tf_op jit(solution)/shard_map/all_gather | solution.py:276
  15.8 706.5 %all-gather.17.cloned.1.call-start = ((), (), s32[]{:S(2)}) async-start(), calls=%async_computation.21 | async-start | bytes 18874368 | tf_op jit(solution)/shard_map/all_gather | solution.py:277
  16.4 1278.1 %reduce-scatter.11.cloned.1.call-start = ((), (), s32[]{:S(2)}) async-start(), calls=%async_computation.14 | async-start | bytes 9437184 | tf_op jit(solution)/shard_map/reduce_scatter | solution.py:297
  39.7 107.9 %copy-start.48 = (f32[1,1,1024]{2,0,1:T(1,128)}, f32[1,1,1024]{2,0,1:T(1,128)S(1)}, u32[]{:S(2)}) copy-start(f32[1,1,1024]{2,0,1:T(1,128)S(1)} %get-tuple-element.465) | copy-start | bytes 12292
  39.8 107.8 %copy-start.105 = (f32[1,1,1024]{2,0,1:T(1,128)}, f32[1,1,1024]{2,0,1:T(1,128)S(1)}, u32[]{:S(2)}) copy-start(f32[1,1,1024]{2,0,1:T(1,128)S(1)} %get-tuple-element.466) | copy-start | bytes 12292
  39.8 260.1 %copy-start.65 = (f32[1,1,1024]{2,0,1:T(1,128)}, f32[1,1,1024]{2,0,1:T(1,128)S(1)}, u32[]{:S(2)}) copy-start(f32[1,1,1024]{2,0,1:T(1,128)S(1)} %get-tuple-element.463) | copy-start | bytes 12292
  39.8 260.1 %copy-start.67 = (f32[1,1,1024]{2,0,1:T(1,128)}, f32[1,1,1024]{2,0,1:T(1,128)S(1)}, u32[]{:S(2)}) copy-start(f32[1,1,1024]{2,0,1:T(1,128)S(1)} %get-tuple-element.464) | copy-start | bytes 12292
  39.8 328.3 %copy-start.78 = (f32[1,1,1024]{2,0,1:T(1,128)}, f32[1,1,1024]{2,0,1:T(1,128)S(1)}, u32[]{:S(2)}) copy-start(f32[1,1,1024]{2,0,1:T(1,128)S(1)} %get-tuple-element.461) | copy-start | bytes 12292
  39.8 328.3 %copy-start.103 = (f32[1,1,1024]{2,0,1:T(1,128)}, f32[1,1,1024]{2,0,1:T(1,128)S(1)}, u32[]{:S(2)}) copy-start(f32[1,1,1024]{2,0,1:T(1,128)S(1)} %get-tuple-element.462) | copy-start | bytes 12292
  39.8 355.4 %copy-start.69 = (f32[1,1,1024]{2,0,1:T(1,128)}, f32[1,1,1024]{2,0,1:T(1,128)S(1)}, u32[]{:S(2)}) copy-start(f32[1,1,1024]{2,0,1:T(1,128)S(1)} %get-tuple-element.459) | copy-start | bytes 12292
  39.8 355.4 %copy-start.109 = (f32[1,1,1024]{2,0,1:T(1,128)}, f32[1,1,1024]{2,0,1:T(1,128)S(1)}, u32[]{:S(2)}) copy-start(f32[1,1,1024]{2,0,1:T(1,128)S(1)} %get-tuple-element.460) | copy-start | bytes 12292
  39.9 328.2 %copy-start.71 = (f32[1,4,1024]{2,0,1:T(1,128)}, f32[1,4,1024]{2,0,1:T(1,128)S(1)}, u32[]{:S(2)}) copy-start(f32[1,4,1024]{2,0,1:T(1,128)S(1)} %slice.263) | copy-start | bytes 49156
  395.2 98.7 %copy-start.80 = (f32[1,1,1024]{2,0,1:T(1,128)S(1)}, f32[1,1,1024]{2,0,1:T(1,128)}, u32[]{:S(2)}) copy-start(f32[1,1,1024]{2,0,1:T(1,128)} %get-tuple-element.455) | copy-start | bytes 12292
  395.2 98.7 %copy-start.92 = (f32[3072]{0:T(1024)S(1)}, f32[3072]{0:T(1024)}, u32[]{:S(2)}) copy-start(f32[3072]{0:T(1024)} %get-tuple-element.475) | copy-start | bytes 36868
  406.7 241.0 %copy-start.5 = (f32[1,520,1024]{2,1,0:T(8,128)}, f32[1,520,1024]{2,1,0:T(8,128)S(1)}, u32[]{:S(2)}) copy-start(f32[1,520,1024]{2,1,0:T(8,128)S(1)} %get-tuple-element.422) | copy-start | bytes 6389764
  652.5 122.0 %copy-start.61 = (f32[520]{0:T(1024)}, f32[520]{0:T(1024)S(1)}, u32[]{:S(2)}) copy-start(f32[520]{0:T(1024)S(1)} %broadcast_multiply_fusion) | copy-start | bytes 6244
  654.4 120.2 %copy-start.88 = (f32[520]{0:T(1024)}, f32[520]{0:T(1024)S(1)}, u32[]{:S(2)}) copy-start(f32[520]{0:T(1024)S(1)} %fusion.202) | copy-start | bytes 6244
  1147.2 299.8 %reduce-scatter.13.cloned.1.call-start = ((), (), s32[]{:S(2)}) async-start(), calls=%async_computation.15 | async-start | bytes 9437184 | tf_op jit(solution)/shard_map/reduce_scatter | solution.py:297
  1167.7 343.8 %all-reduce.12.cloned.1.call-start = ((), (), s32[]{:S(2)}) async-start(), calls=%async_computation.26 | async-start | bytes 4194304 | tf_op jit(solution)/shard_map/psum | solution.py:19
  1447.0 351.4 %reduce-scatter.15.cloned.1.call-start = ((), (), s32[]{:S(2)}) async-start(), calls=%async_computation.16 | async-start | bytes 18874368 | tf_op jit(solution)/shard_map/reduce_scatter | solution.py:300
  1462.8 621.2 %reduce-scatter.17.cloned.1.call-start = ((), (), s32[]{:S(2)}) async-start(), calls=%async_computation.17 | async-start | bytes 18874368 | tf_op jit(solution)/shard_map/reduce_scatter | solution.py:300
  1489.1 659.3 %reduce-scatter.19.cloned.1.call-start = ((), (), s32[]{:S(2)}) async-start(), calls=%async_computation.22 | async-start | bytes 294912
  1503.6 709.5 %reduce-scatter.21.cloned.1.call-start = ((), (), s32[]{:S(2)}) async-start(), calls=%async_computation.23 | async-start | bytes 294912
  1507.0 577.1 %copy-start.13 = (f32[520,1024]{1,0:T(8,128)S(1)}, f32[520,1024]{1,0:T(8,128)}, u32[]{:S(2)}) copy-start(f32[520,1024]{1,0:T(8,128)} %copy-done.12) | copy-start | bytes 6389764
  1507.0 577.1 %copy-start.18 = (bf16[1,520,1024]{2,1,0:T(8,128)(2,1)S(1)}, bf16[1,520,1024]{2,1,0:T(8,128)(2,1)}, u32[]{:S(2)}) copy-start(bf16[1,520,1024]{2,1,0:T(8,128)(2,1)} %param.20) | copy-start | bytes 3194884
  1507.0 728.8 %all-reduce.10.cloned.1.call-start = ((), (), s32[]{:S(2)}) async-start(), calls=%async_computation.25 | async-start | bytes 4194304 | tf_op jit(solution)/shard_map/psum | solution.py:20
  1511.5 813.6 %all-reduce.8.cloned.1.call-start = ((), (), s32[]{:S(2)}) async-start(), calls=%async_computation.24 | async-start | bytes 8388608 | tf_op jit(solution)/shard_map/psum | solution.py:309
  2084.1 135.6 %copy-start.46 = (bf16[2,14,128]{2,0,1:T(2,128)(2,1)S(1)}, bf16[2,14,128]{2,0,1:T(2,128)(2,1)}, u32[]{:S(2)}) copy-start(bf16[2,14,128]{2,0,1:T(2,128)(2,1)} %param.24) | copy-start | bytes 21508
  2084.1 135.6 %copy-start.90 = (f32[2,14,128]{2,0,1:T(2,128)S(1)}, f32[2,14,128]{2,0,1:T(2,128)}, u32[]{:S(2)}) copy-start(f32[2,14,128]{2,0,1:T(2,128)} %param.30) | copy-start | bytes 43012
  2084.1 135.6 %copy-start.91 = (f32[2,14,128]{2,0,1:T(2,128)S(1)}, f32[2,14,128]{2,0,1:T(2,128)}, u32[]{:S(2)}) copy-start(f32[2,14,128]{2,0,1:T(2,128)} %param.31) | copy-start | bytes 43012
  (116 other events, 1923.4 us)
Sparse Core Ops, SparseCore 0:
  10.7 128.7 all-gather.10
  142.2 225.7 all-gather.12
  370.8 123.1 all-gather.14
  496.5 225.7 all-gather.16
  1147.3 147.1 reduce-scatter.10
  1299.0 147.9 reduce-scatter.12
  1449.4 62.0 all-reduce.11
  1515.7 282.6 reduce-scatter.14
  1802.2 281.7 reduce-scatter.16
  2088.1 60.3 reduce-scatter.18
  2152.8 60.2 reduce-scatter.20
  2215.4 20.3 all-reduce.9
  2238.2 86.8 all-reduce.7
